TPU v7x, 32 devices: a whole 2x2x4 slice. The times are simulated.
32 devices in a mesh: seq: 8 (over z, x), tp: 4 (over y, core).
Axes of the slice: x: 2, y: 2, z: 4, core: 2. Of those that a mesh axis runs over, the one named last changes fastest.
Arguments:
- hidden_in: bfloat16 [4, 24, 3072], P(None, None, 'seq'), may hold values from -30 to 30
- attn_gain: bfloat16 [3072], P('seq'), may hold values from 0.5 to 1.5
- w_query: bfloat16 [3072, 3072], P('seq', 'tp'), may hold values from -0.109375 to 0.109375
- w_key: bfloat16 [3072, 3072], P('seq', 'tp'), may hold values from -0.109375 to 0.109375
- w_value: bfloat16 [3072, 3072], P('seq', 'tp'), may hold values from -0.109375 to 0.109375
- w_out: bfloat16 [3072, 3072], P('tp', 'seq'), may hold values from -0.109375 to 0.109375
- mlp_gain: bfloat16 [3072], P('seq'), may hold values from 0.5 to 1.5
- w_gate: bfloat16 [3072, 8192], P('seq', 'tp'), may hold values from -0.109375 to 0.109375
- w_up: bfloat16 [3072, 8192], P('seq', 'tp'), may hold values from -0.109375 to 0.109375
- w_down: bfloat16 [8192, 3072], P('tp', 'seq'), may hold values from -0.0625 to 0.0625
- kv_pages: bfloat16 [2, 1664, 32, 3072], P(None, 'seq', None, 'tp'), may hold values from -260 to 260
- lengths: int32 [24], replicated, may hold values from 512 to 2044, as said below
- group_ids: int32 [24], replicated, may hold values from 0 to 1, as said below
- shared_table: int32 [2, 16], replicated, may hold values from 0 to 207, as said below
- own_table: int32 [24, 64], P(None, 'seq'), may hold values from 0 to 207, as said below
Outputs:
- hidden_out: bfloat16 [4, 24, 3072], P(None, None, 'seq')
- new_cache: bfloat16 [2, 4, 24, 3072], P(None, None, None, 'tp')
Inputs may be any that keep to these rules, and one draw needn't show every extreme that they name: `lengths`: one request in every draw has the length 2044. `group_ids`: each group number is named by exactly 12 requests. Entries are pages of the pool of the index of seq that holds the page's positions (prompt page p lies on index p // 8); on one index the pages named by shared_table and own_table are all different. `own_table`: entries are pages of the pool of the index of seq that holds the page's positions; entries of logical pages under 16 are never read.
All inputs are finite; a program needn't handle non-finite values.
Results may differ from a plain program's by a relative error of at most 0.0085.
The roundings to bfloat16 on the way count: a program that leaves them out, or rounds other values in their place, can miss the bound.
Values may be sent and summed in bfloat16 or wider, within the bound.
A program may use at most 192 MiB of HBM per device.

v0:
```python
import math
import jax
import jax.numpy as jnp
from jax import lax
from jax.sharding import PartitionSpec as P

D = 3072
HEAD_DIM = 96
SINKS = 4
WINDOW = 1024
EPSILON = 1e-05
ROPE_BASE = 10000.0
NEGATIVE = -1e30


def rotate(vector, position):
    halfway = vector.shape[-1] // 2
    frequency = ROPE_BASE ** (-(jnp.arange(halfway, dtype=jnp.float32) * 2.0 / vector.shape[-1]))
    angles = position[..., None].astype(jnp.float32) * frequency
    cosine = jnp.cos(angles)
    sine_part = jnp.sin(angles)
    first_half = vector[..., :halfway]
    second_half = vector[..., halfway:]
    return jnp.concatenate(
        [
            first_half * cosine - second_half * sine_part,
            second_half * cosine + first_half * sine_part,
        ],
        -1,
    )


def seq_total(partial_value, squares):
    return lax.psum((partial_value, squares), "seq")


def head_total(partial_value):
    return lax.psum(partial_value, "tp")


def body(
    hidden_in,
    attn_gain,
    w_query,
    w_key,
    w_value,
    w_out,
    mlp_gain,
    w_gate,
    w_up,
    w_down,
    kv_pages,
    lengths,
    group_ids,
    shared_table,
    own_table,
):
    seq_index = lax.axis_index("seq")
    step_count = hidden_in.shape[0]
    requests = hidden_in.shape[1]
    local_width = hidden_in.shape[2]
    head_cols = w_query.shape[1]
    local_heads = head_cols // HEAD_DIM
    unit_cols = w_gate.shape[1]
    page_rows = kv_pages.shape[2]
    local_pages = own_table.shape[1]
    block_len = local_pages * page_rows
    group_count = shared_table.shape[0]
    prompt_pages = shared_table.shape[1]
    score_scale = 1.0 / math.sqrt(HEAD_DIM)
    flat_rows = step_count * requests
    logical = seq_index * local_pages + jnp.arange(local_pages, dtype=jnp.int32)
    group_pick = (group_ids[:, None] == jnp.arange(group_count, dtype=jnp.int32)[None, :]).astype(
        jnp.int32
    )
    group_rows = jnp.sum(group_pick[:, :, None] * shared_table[None, :, :], axis=1)
    column_pick = (logical[:, None] == jnp.arange(prompt_pages, dtype=jnp.int32)[None, :]).astype(
        jnp.int32
    )
    shared_local = jnp.sum(group_rows[:, None, :] * column_pick[None, :, :], axis=2)
    physical = jnp.where(logical[None, :] < prompt_pages, shared_local, own_table)
    gathered = kv_pages[:, physical]
    cached_keys = gathered[0].reshape(requests, block_len, local_heads, HEAD_DIM)
    cached_values = (
        gathered[1].reshape(requests, block_len, local_heads, HEAD_DIM).astype(jnp.float32)
    )
    positions = seq_index * block_len + jnp.arange(block_len, dtype=jnp.int32)
    step_ids = jnp.arange(step_count, dtype=jnp.int32)
    owner_new = jnp.transpose((lengths[None, :] + step_ids[:, None]) // block_len == seq_index)
    attn_scale = attn_gain.astype(jnp.float32)
    mlp_scale = mlp_gain.astype(jnp.float32)
    w_pair = jnp.concatenate([w_gate, w_up], axis=1)
    residual = hidden_in.astype(jnp.float32).reshape(flat_rows, local_width)
    normed = (residual * attn_scale).astype(jnp.bfloat16)
    squares = jnp.sum(residual * residual, axis=-1)
    where_now = lengths[None, :] + step_ids[:, None]
    w_qkv = jnp.concatenate([w_query, w_key, w_value], axis=1)
    partial_value = jnp.dot(normed, w_qkv, preferred_element_type=jnp.float32)
    summed, square_sum = seq_total(partial_value, squares)
    inv_rms = lax.rsqrt(square_sum / D + EPSILON)
    projected = (summed * inv_rms[:, None]).reshape(step_count, requests, 3, local_heads, HEAD_DIM)
    queries = rotate(projected[:, :, 0], where_now[:, :, None]).astype(jnp.bfloat16)
    key_new = (
        rotate(projected[:, :, 1], where_now[:, :, None])
        .astype(jnp.bfloat16)
        .reshape(step_count, requests, head_cols)
    )
    value_new = projected[:, :, 2].astype(jnp.bfloat16).reshape(step_count, requests, head_cols)
    store_keys = key_new.reshape(step_count, requests, local_heads, HEAD_DIM)
    store_values = value_new.reshape(step_count, requests, local_heads, HEAD_DIM).astype(
        jnp.float32
    )
    in_window = positions[None, None, :] > lengths[None, :, None] + step_ids[:, None, None] - WINDOW
    is_live = (positions[None, None, :] < lengths[None, :, None]) & (
        (positions[None, None, :] < SINKS) | in_window
    )
    new_live = (step_ids[None, None, :] <= step_ids[:, None, None]) & owner_new[None, :, :]
    scores = (
        jnp.einsum("tbhd,bkhd->tbhk", queries, cached_keys, preferred_element_type=jnp.float32)
        * score_scale
    )
    new_scores = (
        jnp.einsum("tbhd,sbhd->tbhs", queries, store_keys, preferred_element_type=jnp.float32)
        * score_scale
    )
    scores = jnp.where(is_live[:, :, None, :], scores, NEGATIVE)
    new_scores = jnp.where(new_live[:, :, None, :], new_scores, NEGATIVE)
    local_peak = jnp.maximum(jnp.max(scores, axis=-1), jnp.max(new_scores, axis=-1))
    score_peak = lax.pmax(local_peak, "seq")
    weights = jnp.where(is_live[:, :, None, :], jnp.exp(scores - score_peak[..., None]), 0.0)
    new_weights = jnp.where(
        new_live[:, :, None, :], jnp.exp(new_scores - score_peak[..., None]), 0.0
    )
    weight_sum = jnp.sum(weights, axis=-1) + jnp.sum(new_weights, axis=-1)
    weighted = jnp.einsum("tbhk,bkhd->tbhd", weights, cached_values) + jnp.einsum(
        "tbhs,sbhd->tbhd", new_weights, store_values
    )
    local_sum = weight_sum
    local_weighted = weighted
    weight_sum, weighted = lax.psum((local_sum, local_weighted), "seq")
    attn = (weighted / weight_sum[..., None]).astype(jnp.bfloat16).reshape(flat_rows, head_cols)
    mid_rows = residual + head_total(jnp.dot(attn, w_out, preferred_element_type=jnp.float32))
    mlp_in = (mid_rows * mlp_scale).astype(jnp.bfloat16)
    mid_squares = jnp.sum(mid_rows * mid_rows, axis=-1)
    gate_up = jnp.dot(mlp_in, w_pair, preferred_element_type=jnp.float32)
    pair_sum, mid_sum = seq_total(gate_up, mid_squares)
    inv_mid = lax.rsqrt(mid_sum / D + EPSILON)[:, None]
    activated = (
        jax.nn.silu(pair_sum[:, :unit_cols] * inv_mid) * (pair_sum[:, unit_cols:] * inv_mid)
    ).astype(jnp.bfloat16)
    result = (
        mid_rows + head_total(jnp.dot(activated, w_down, preferred_element_type=jnp.float32))
    ).astype(jnp.bfloat16)
    hidden_out = result.reshape(step_count, requests, local_width)
    return (hidden_out, jnp.stack([key_new, value_new]))


def solution(mesh):
    return jax.shard_map(
        body,
        mesh=mesh,
        in_specs=(
            P(None, None, "seq"),
            P("seq"),
            P("seq", "tp"),
            P("seq", "tp"),
            P("seq", "tp"),
            P("tp", "seq"),
            P("seq"),
            P("seq", "tp"),
            P("seq", "tp"),
            P("tp", "seq"),
            P(None, "seq", None, "tp"),
            P(),
            P(),
            P(),
            P(None, "seq"),
        ),
        out_specs=(P(None, None, "seq"), P(None, None, None, "tp")),
        check_vma=False,
    )
```

profile of v0, /device:TPU:0, one launch (start us, length us, event | category | flops | bytes accessed | tf_op | source)
XLA Modules:
  0.0 413.2 jit_solution(18278633913271878751)
XLA Ops:
  7.2 0.0 all-reduce.6.cloned.1.call-start
  7.3 0.8 convert_element_type.82
  8.1 0.9 fusion.40
  9.0 2.8 fusion.8
  11.7 0.0 all-reduce.6.cloned.1.call-update
  11.7 0.0 all-reduce.8.cloned.1.call-start
  11.8 0.1 fusion.39
  12.0 0.1 fusion.48
  12.1 0.1 multiply_reduce_fusion.2
  12.2 0.1 multiply_reduce_fusion.1
  12.3 0.1 compare_select_fusion
  12.3 0.1 copy.33
  12.4 0.1 reshape.251
  12.5 17.1 %gather_fusion = bf16[192,2,32,768]{3,2,1,0:T(8,128)(2,1)} fusion(bf16[2,208,32,768]{3,2,1,0:T(8,128)(2,1)} %param.25, s32[1024]{0:T(1024)S(1)} %pad_clamp_fusion), kind=kCustom, calls=%fused_computation | custom fusion | bytes 37749504 | tf_op jit(solution)/shard_map/gather | solution.py:82
  29.7 9.6 %copy.69 = bf16[24,8,2,32,768]{4,3,1,0,2:T(8,128)(2,1)S(1)} copy(bf16[24,8,2,32,768]{4,3,2,1,0:T(8,128)(2,1)} %bitcast.48) | data formatting | bytes 37748736 | tf_op jit(solution)/shard_map/gather | solution.py:82
  39.2 6.9 %fusion.55 = (bf16[1,24,8,32,768]{4,3,2,1,0:T(8,128)(2,1)}, bf16[1,24,8,32,768]{4,3,2,1,0:T(8,128)(2,1)}) fusion(bf16[2,24,8,32,768]{4,3,2,1,0:T(8,128)(2,1)S(1)} %bitcast.47), kind=kLoop, calls=%fused_computation.100 | loop fusion | bytes 37748736 | tf_op jit(solution)/shard_map/slice | solution.py:83
  46.1 21.8 %reshape_squeeze.6 = bf16[24,256,8,96]{3,2,1,0:T(8,128)(2,1)} reshape(bf16[1,24,8,32,768]{4,3,2,1,0:T(8,128)(2,1)} %get-tuple-element.3) | data formatting | bytes 18874368 | tf_op jit(solution)/shard_map/reshape;squeeze | solution.py:85
  67.9 0.1 reduce_sum.59
  68.0 23.8 %psum.57 = f32[96]{0:T(128)S(1)} all-reduce(f32[96]{0:T(128)S(1)} %reduce_sum.59), channel_id=1, replica_groups=mesh['seq'=8,'tp'=4] {'seq'}, use_global_device_ids=true, to_apply=%region_4.5 | all-reduce | flops 96 | bytes 768 | tf_op jit(solution)/shard_map/psum | solution.py:34
  91.8 21.8 %reshape_squeeze.7 = bf16[24,256,8,96]{3,2,1,0:T(8,128)(2,1)} reshape(bf16[1,24,8,32,768]{4,3,2,1,0:T(8,128)(2,1)} %get-tuple-element.2) | data formatting | bytes 18874368 | tf_op jit(solution)/shard_map/reshape;squeeze | solution.py:83
  113.5 0.1 fusion.43
  113.6 0.1 broadcast_compare_fusion
  113.7 0.1 broadcast_and_fusion
  113.8 0.1 fusion.45
  113.9 0.1 or_and_fusion
  114.0 0.4 multiply_cosine_fusion
  114.4 0.0 all-reduce.6.cloned.1.call-done
  114.4 2.3 broadcast_multiply_fusion
  116.7 2.0 reshape.246
  118.7 0.1 fusion.56
  118.8 0.5 copy_bitcast_fusion.1
  119.3 0.4 subtract_convert_fusion
  119.7 0.4 multiply_subtract_fusion
  120.1 0.3 maximum_convert_fusion
  120.3 0.0 copy-done.3
  120.4 0.1 copy-done.4
  120.4 8.1 %fusion.57 = (f32[4,24,8]{0,2,1:T(8,128)S(1)}, f32[4,24,8,256]{3,0,2,1:T(4,128)S(1)}) fusion(bf16[4,24,8,48]{3,0,2,1:T(4,128)(2,1)S(1)} %get-tuple-element.9, bf16[4,24,8,48]{3,0,2,1:T(4,128)(2,1)S(1)} %get-tuple-element.8, bf16[24,256,8,96]{3,2,1,0:T(8,128)(2,1)} %reshape_squeeze.7, pred[4,24,256]{2,0,1:T(4,128)(4,1)S(1)} %or_and_fusion), kind=kOutput, calls=%fused_computation.102 | convolution fusion | flops 38632704 | bytes 10398720 | tf_op jit(solution)/shard_map/tbhd,bkhd->tbhk/dot_general | solution.py:119
  128.5 1.6 fusion.58
  130.2 33.8 %pmax.7 = f32[4,24,8]{0,2,1:T(8,128)S(1)} all-reduce(f32[4,24,8]{0,2,1:T(8,128)S(1)} %max.5), channel_id=1, replica_groups=mesh['seq'=8,'tp'=4] {'seq'}, use_global_device_ids=true, to_apply=%region_7.8 | all-reduce | flops 768 | bytes 6144 | tf_op jit(solution)/shard_map/pmax | solution.py:129
  164.0 7.2 %fusion = f32[24,8,96,4]{2,3,1,0:T(4,128)} fusion(bf16[24,256,8,96]{3,2,1,0:T(8,128)(2,1)} %reshape_squeeze.6, f32[4,24,8,256]{3,0,2,1:T(4,128)S(1)} %get-tuple-element.17, f32[4,24,8]{0,2,1:T(8,128)S(1)} %pmax.7, pred[4,24,256]{2,0,1:T(4,128)(4,1)S(1)} %or_and_fusion), kind=kOutput, calls=%fused_computation.2 | convolution fusion | flops 38141952 | bytes 10546176 | tf_op jit(solution)/shard_map/tbhk,bkhd->tbhd/dot_general | solution.py:135
  171.1 2.3 fusion.21
  173.4 0.0 all-reduce.8.cloned.1.call-update
  173.4 0.0 all-reduce.10.cloned.1.call-start
  173.5 0.4 fusion.34
  173.9 0.6 fusion.28
  174.5 36.2 %psum.59 = f32[4,24,8]{0,2,1:T(8,128)S(1)} all-reduce(f32[4,24,8]{0,2,1:T(8,128)S(1)} %add.156), channel_id=1, replica_groups=mesh['seq'=8,'tp'=4] {'seq'}, use_global_device_ids=true, to_apply=%region_11.12 | all-reduce | flops 768 | bytes 6144 | tf_op jit(solution)/shard_map/psum | solution.py:140
  210.7 33.2 %all-reduce.8.cloned.1.call-done = f32[4,24,8,96]{3,0,2,1:T(4,128)} async-done(((f32[4,24,8,96]{3,0,2,1:T(4,128)}), f32[4,24,8,96]{3,0,2,1:T(4,128)}) %all-reduce.8.cloned.1.call-update) | async-done | bytes 294928 | tf_op jit(solution)/shard_map/psum | solution.py:140
  243.9 1.3 divide_convert_fusion
  245.2 0.2 reshape.247
  245.4 2.0 fusion.59
  247.4 0.0 all-reduce.10.cloned.1.call-update
  247.4 0.0 all-reduce.12.cloned.1.call-start
  247.5 29.9 %all-reduce.10.cloned.1.call-done = f32[96,384]{1,0:T(8,128)} async-done(((f32[96,384]{1,0:T(8,128)}), f32[96,384]{1,0:T(8,128)}) %all-reduce.10.cloned.1.call-update) | async-done | bytes 147472 | tf_op jit(solution)/shard_map/psum | solution.py:38
  277.4 1.0 multiply_reduce_fusion
  278.4 3.8 fusion.4
  282.2 0.0 all-reduce.14.cloned.1.call-start
  282.2 0.2 convert_element_type.94
  282.5 0.2 convert_element_type.93
  282.6 22.1 %psum.62 = f32[96]{0:T(128)S(1)} all-reduce(f32[96]{0:T(128)S(1)} %get-tuple-element.10), channel_id=1, replica_groups=mesh['seq'=8,'tp'=4] {'seq'}, use_global_device_ids=true, to_apply=%region_15.16 | all-reduce | flops 96 | bytes 768 | tf_op jit(solution)/shard_map/psum | solution.py:34
  304.8 67.5 %all-reduce.12.cloned.1.call-done = f32[96,4096]{1,0:T(8,128)} async-done(((f32[96,4096]{1,0:T(8,128)}), f32[96,4096]{1,0:T(8,128)}) %all-reduce.12.cloned.1.call-update) | async-done | bytes 1572880 | tf_op jit(solution)/shard_map/psum | solution.py:34
  372.3 2.5 fusion.32
  374.8 0.7 pad_maximum_fusion
  375.6 29.5 %all-reduce.14.cloned.1.call-done = f32[96,384]{1,0:T(8,128)} async-done(((f32[96,384]{1,0:T(8,128)}), f32[96,384]{1,0:T(8,128)}) %all-reduce.14.cloned.1.call-update) | async-done | bytes 147472 | tf_op jit(solution)/shard_map/psum | solution.py:38
  405.1 1.6 add_convert_fusion.1
  (36 shorter events, 0.3 us)
Async XLA Ops:
  7.2 365.1 %copy-start = (bf16[2048,384]{1,0:T(8,128)(2,1)S(1)}, bf16[2048,384]{1,0:T(8,128)(2,1)}, u32[]{:S(2)}) copy-start(bf16[2048,384]{1,0:T(8,128)(2,1)} %param.24) | copy-start | bytes 4718596
  7.2 4.7 %copy-start.1 = (bf16[4,24,384]{2,1,0:T(8,128)(2,1)S(1)}, bf16[4,24,384]{2,1,0:T(8,128)(2,1)}, u32[]{:S(2)}) copy-start(bf16[4,24,384]{2,1,0:T(8,128)(2,1)} %param.15) | copy-start | bytes 221188
  7.2 4.9 %copy-start.9 = (s32[24]{0:T(128)S(1)}, s32[24]{0:T(128)}, u32[]{:S(2)}) copy-start(s32[24]{0:T(128)} %param.27) | copy-start | bytes 292
  7.2 4.9 %copy-start.7 = (s32[2,16]{1,0:T(2,128)S(1)}, s32[2,16]{1,0:T(2,128)}, u32[]{:S(2)}) copy-start(s32[2,16]{1,0:T(2,128)} %param.28) | copy-start | bytes 388
  7.2 5.0 %copy-start.6 = (s32[24,8]{0,1:T(8,128)S(1)}, s32[24,8]{0,1:T(8,128)}, u32[]{:S(2)}) copy-start(s32[24,8]{0,1:T(8,128)} %param.29) | copy-start | bytes 2308
  7.2 107.2 %all-reduce.6.cloned.1.call-start = ((), (), s32[]{:S(2)}) async-start(), calls=%async_computation | async-start | bytes 1769472 | tf_op jit(solution)/shard_map/psum | solution.py:34
  11.7 232.2 %all-reduce.8.cloned.1.call-start = ((), (), s32[]{:S(2)}) async-start(), calls=%async_computation.1 | async-start | bytes 786432 | tf_op jit(solution)/shard_map/psum | solution.py:140
  91.8 21.8 %copy-start.5 = (s32[24]{0:T(128)S(1)}, s32[24]{0:T(128)}, u32[]{:S(2)}) copy-start(s32[24]{0:T(128)} %param.26) | copy-start | bytes 292
  119.7 0.7 copy-start.3
  119.7 0.7 copy-start.4
  171.1 76.4 %copy-start.8 = (bf16[384]{0:T(512)(128)(2,1)S(1)}, bf16[384]{0:T(512)(128)(2,1)}, u32[]{:S(2)}) copy-start(bf16[384]{0:T(512)(128)(2,1)} %param.21) | copy-start | bytes 2308
  173.4 104.0 %all-reduce.10.cloned.1.call-start = ((), (), s32[]{:S(2)}) async-start(), calls=%async_computation.2 | async-start | bytes 294912 | tf_op jit(solution)/shard_map/psum | solution.py:38
  247.4 124.9 %all-reduce.12.cloned.1.call-start = ((), (), s32[]{:S(2)}) async-start(), calls=%async_computation.3 | async-start | bytes 3145728 | tf_op jit(solution)/shard_map/psum | solution.py:34
  282.2 122.9 %all-reduce.14.cloned.1.call-start = ((), (), s32[]{:S(2)}) async-start(), calls=%async_computation.4 | async-start | bytes 294912 | tf_op jit(solution)/shard_map/psum | solution.py:38
  282.4 122.7 %copy-start.2 = (f32[96,384]{1,0:T(8,128)S(1)}, f32[96,384]{1,0:T(8,128)}, u32[]{:S(2)}) copy-start(f32[96,384]{1,0:T(8,128)} %all-reduce.10.cloned.1.call-done) | copy-start | bytes 442372
Sparse Core Ops, SparseCore 0:
  11.9 78.9 all-reduce.5
  173.5 70.3 all-reduce.7
  247.5 29.7 all-reduce.9
  282.3 89.9 all-reduce.11
  374.9 30.1 all-reduce.13
where the time goes:
time: 415 us; the launch traced here: 413 us
  waiting for transfers between devices  160 us (39%)
  blocking collectives  116 us (28%)
  local copies, waits for them, and re-layouts  80.6 us (19%)
  matrix products  30.1 us (7%)
  between operations  14.1 us (3%)
  other arithmetic  11.9 us (3%)
    psum x2, waiting for transfers between devices, seq_total(): return lax.psum((partial_value, squares), 'seq')  67.6 us
    psum x2, waiting for transfers between devices, head_total(): return lax.psum(partial_value, 'tp')  59.4 us
    psum x2, blocking collectives, seq_total(): return lax.psum((partial_value, squares), 'seq')  45.9 us
    psum x1, blocking collectives, body(): weight_sum, weighted = lax.psum((local_sum, local_weighted), 'seq')  36.2 us
    pmax x1, blocking collectives, body(): score_peak = lax.pmax(local_peak, 'seq')  33.8 us
    psum x1, waiting for transfers between devices, body(): weight_sum, weighted = lax.psum((local_sum, local_weighted), 'seq')  33.2 us
    gather x2, local copies, waits for them, and re-layouts, body(): gathered = kv_pages[:, physical]  26.7 us
    another operation x1, local copies, waits for them, and re-layouts, body(): gathered[1].reshape(requests, block_len, local_heads, HEAD_DIM)  21.8 us
  transfers between devices with their start and end apart: 5, of which 4 were waited for; matrix products, arithmetic and copies ran while one was open for 20% of the time, Pallas kernels for 0%

commit v1 on v0

--- a/solution.py
+++ b/solution.py
@@ -35,7 +35,7 @@
 
 
 def head_total(partial_value):
-    return lax.psum(partial_value, "tp")
+    return jnp.sum(lax.all_gather(partial_value, "tp"), axis=0)
 
 
 def body(

time: 415 us -> 362 us (0.87)
  waiting for transfers between devices: 160 us -> 98.6 us
  blocking collectives: 116 us -> 129 us
    psum x2 -> x0, waiting for transfers between devices: 59.4 us -> none  [head_total(): return lax.psum(partial_value, 'tp')]
    all_gather x0 -> x2, blocking collectives: none -> 15 us  [head_total(): return jnp.sum(lax.all_gather(partial_value, 'tp'), axis=0)]
  transfers between devices with their start and end apart: 5 -> 3, of which waited for: 4 -> 2; matrix products, arithmetic and copies ran while one was open for 20% -> 23% of each run, Pallas kernels for 0% -> 0%
where the time goes in v1:
time: 362 us; the launch traced here: 360 us
  blocking collectives  129 us (36%)
  waiting for transfers between devices  98.6 us (27%)
  local copies, waits for them, and re-layouts  80.6 us (22%)
  matrix products  27 us (7%)
  between operations  14.1 us (4%)
  other arithmetic  11.2 us (3%)
    psum x2, waiting for transfers between devices, seq_total(): return lax.psum((partial_value, squares), 'seq')  66.2 us
    psum x2, blocking collectives, seq_total(): return lax.psum((partial_value, squares), 'seq')  44 us
    psum x1, blocking collectives, body(): weight_sum, weighted = lax.psum((local_sum, local_weighted), 'seq')  35.9 us
    pmax x1, blocking collectives, body(): score_peak = lax.pmax(local_peak, 'seq')  33.8 us
    psum x1, waiting for transfers between devices, body(): weight_sum, weighted = lax.psum((local_sum, local_weighted), 'seq')  32.3 us
    gather x2, local copies, waits for them, and re-layouts, body(): gathered = kv_pages[:, physical]  26.7 us
    another operation x1, local copies, waits for them, and re-layouts, body(): gathered[0].reshape(requests, block_len, local_heads, HEAD_DIM)  21.8 us
    another operation x1, local copies, waits for them, and re-layouts, body(): gathered[1].reshape(requests, block_len, local_heads, HEAD_DIM)  21.8 us
  transfers between devices with their start and end apart: 3, of which 2 were waited for; matrix products, arithmetic and copies ran while one was open for 23% of the time, Pallas kernels for 0%

profile of v1, /device:TPU:0, one launch (start us, length us, event | category | flops | bytes accessed | tf_op | source)
XLA Modules:
  0.0 360.4 jit_solution(15576846472849950109)
XLA Ops:
  7.2 0.0 copy-start
  7.2 0.0 copy-start.1
  7.2 0.0 all-reduce.4.cloned.1.call-start
  7.3 0.8 convert_element_type.83
  8.1 0.9 fusion.40
  9.0 2.8 fusion.8
  11.7 0.0 all-reduce.4.cloned.1.call-update
  11.7 0.0 all-reduce.6.cloned.1.call-start
  11.8 0.0 copy-done.1
  11.8 0.1 fusion.39
  12.0 0.1 fusion.49
  12.1 0.1 multiply_reduce_fusion.2
  12.2 0.1 multiply_reduce_fusion.1
  12.3 0.1 compare_select_fusion
  12.3 0.1 copy.33
  12.4 0.1 reshape.252
  12.5 17.1 %gather_fusion = bf16[192,2,32,768]{3,2,1,0:T(8,128)(2,1)} fusion(bf16[2,208,32,768]{3,2,1,0:T(8,128)(2,1)} %param.25, s32[1024]{0:T(1024)S(1)} %pad_clamp_fusion), kind=kCustom, calls=%fused_computation | custom fusion | bytes 37749504 | tf_op jit(solution)/shard_map/gather | solution.py:82
  29.7 9.6 %copy.69 = bf16[24,8,2,32,768]{4,3,1,0,2:T(8,128)(2,1)S(1)} copy(bf16[24,8,2,32,768]{4,3,2,1,0:T(8,128)(2,1)} %bitcast.52) | data formatting | bytes 37748736 | tf_op jit(solution)/shard_map/gather | solution.py:82
  39.2 6.9 %fusion.56 = (bf16[1,24,8,32,768]{4,3,2,1,0:T(8,128)(2,1)}, bf16[1,24,8,32,768]{4,3,2,1,0:T(8,128)(2,1)}) fusion(bf16[2,24,8,32,768]{4,3,2,1,0:T(8,128)(2,1)S(1)} %bitcast.51), kind=kLoop, calls=%fused_computation.101 | loop fusion | bytes 37748736 | tf_op jit(solution)/shard_map/slice | solution.py:83
  46.1 21.8 %reshape_squeeze.6 = bf16[24,256,8,96]{3,2,1,0:T(8,128)(2,1)} reshape(bf16[1,24,8,32,768]{4,3,2,1,0:T(8,128)(2,1)} %get-tuple-element.3) | data formatting | bytes 18874368 | tf_op jit(solution)/shard_map/reshape;squeeze | solution.py:85
  67.9 0.1 reduce_sum.83
  68.0 23.8 %psum.43 = f32[96]{0:T(128)S(1)} all-reduce(f32[96]{0:T(128)S(1)} %reduce_sum.83), channel_id=1, replica_groups=mesh['seq'=8,'tp'=4] {'seq'}, use_global_device_ids=true, to_apply=%region_4.5 | all-reduce | flops 96 | bytes 768 | tf_op jit(solution)/shard_map/psum | solution.py:34
  91.8 21.8 %reshape_squeeze.7 = bf16[24,256,8,96]{3,2,1,0:T(8,128)(2,1)} reshape(bf16[1,24,8,32,768]{4,3,2,1,0:T(8,128)(2,1)} %get-tuple-element.2) | data formatting | bytes 18874368 | tf_op jit(solution)/shard_map/reshape;squeeze | solution.py:83
  113.5 0.1 fusion.44
  113.6 0.1 broadcast_compare_fusion
  113.7 0.1 broadcast_and_fusion
  113.8 0.1 fusion.46
  113.9 0.1 or_and_fusion
  114.0 0.4 multiply_cosine_fusion
  114.4 0.0 all-reduce.4.cloned.1.call-done
  114.5 2.3 broadcast_multiply_fusion
  116.7 2.0 reshape.248
  118.7 0.1 fusion.57
  118.8 0.5 copy_bitcast_fusion.1
  119.3 0.4 subtract_convert_fusion
  119.7 0.4 multiply_subtract_fusion
  120.1 0.3 maximum_convert_fusion
  120.3 9.0 %fusion.58 = (f32[4,24,8]{0,2,1:T(8,128)S(1)}, f32[4,24,8,256]{3,0,2,1:T(4,128)}) fusion(bf16[4,24,8,48]{3,0,2,1:T(4,128)(2,1)S(1)} %get-tuple-element.9, bf16[4,24,8,48]{3,0,2,1:T(4,128)(2,1)S(1)} %get-tuple-element.8, bf16[24,256,8,96]{3,2,1,0:T(8,128)(2,1)} %reshape_squeeze.7, pred[4,24,256]{2,0,1:T(4,128)(4,1)S(1)} %or_and_fusion), kind=kOutput, calls=%fused_computation.103 | convolution fusion | flops 38632704 | bytes 10398720 | tf_op jit(solution)/shard_map/tbhd,bkhd->tbhk/dot_general | solution.py:119
  129.3 0.6 fusion.59
  129.9 33.8 %pmax.7 = f32[4,24,8]{0,2,1:T(8,128)S(1)} all-reduce(f32[4,24,8]{0,2,1:T(8,128)S(1)} %max.5), channel_id=1, replica_groups=mesh['seq'=8,'tp'=4] {'seq'}, use_global_device_ids=true, to_apply=%region_7.8 | all-reduce | flops 768 | bytes 6144 | tf_op jit(solution)/shard_map/pmax | solution.py:129
  163.7 6.5 %fusion = f32[24,8,96,4]{2,3,1,0:T(4,128)S(1)} fusion(bf16[24,256,8,96]{3,2,1,0:T(8,128)(2,1)} %reshape_squeeze.6, f32[4,24,8,256]{3,0,2,1:T(4,128)} %get-tuple-element.15, f32[4,24,8]{0,2,1:T(8,128)S(1)} %pmax.7, pred[4,24,256]{2,0,1:T(4,128)(4,1)S(1)} %or_and_fusion), kind=kOutput, calls=%fused_computation.2 | convolution fusion | flops 38141952 | bytes 10546176 | tf_op jit(solution)/shard_map/tbhk,bkhd->tbhd/dot_general | solution.py:135
  170.2 1.2 fusion.21
  171.5 0.0 all-reduce.6.cloned.1.call-update
  171.5 0.0 all-reduce.8.cloned.1.call-start
  171.6 0.4 fusion.34
  172.0 1.7 fusion.28
  173.7 35.9 %psum.45 = f32[4,24,8]{0,2,1:T(8,128)S(1)} all-reduce(f32[4,24,8]{0,2,1:T(8,128)S(1)} %add.157), channel_id=1, replica_groups=mesh['seq'=8,'tp'=4] {'seq'}, use_global_device_ids=true, to_apply=%region_11.12 | all-reduce | flops 768 | bytes 6144 | tf_op jit(solution)/shard_map/psum | solution.py:140
  209.6 32.3 %all-reduce.6.cloned.1.call-done = f32[4,24,8,96]{3,0,2,1:T(4,128)} async-done(((f32[4,24,8,96]{3,0,2,1:T(4,128)}), f32[4,24,8,96]{3,0,2,1:T(4,128)}) %all-reduce.6.cloned.1.call-update) | async-done | bytes 294928 | tf_op jit(solution)/shard_map/psum | solution.py:140
  241.9 1.3 divide_convert_fusion
  243.2 0.2 reshape.249
  243.4 1.3 fusion.60
  244.7 7.5 %all-gather = f32[384,384]{1,0:T(8,128)S(1)} all-gather(f32[96,384]{1,0:T(8,128)S(1)} %fusion.60), channel_id=2, replica_groups=mesh['seq'=8,'tp'=4] {'tp'}, dimensions={0}, use_global_device_ids=true | all-gather | bytes 737280 | tf_op jit(solution)/shard_map/all_gather | solution.py:38
  252.3 3.8 %fusion.4 = f32[96,4096]{1,0:T(8,128)} fusion(bf16[96,384]{1,0:T(8,128)(2,1)S(1)} %fusion.42, bf16[384,2048]{1,0:T(8,128)(2,1)} %param.23, bf16[384,2048]{1,0:T(8,128)(2,1)} %param.22), kind=kOutput, calls=%fused_computation.6 | convolution fusion | flops 308281344 | bytes 4792320 | tf_op jit(solution)/shard_map/dot_general | solution.py:145
  256.1 0.0 all-reduce.8.cloned.1.call-update
  256.1 0.2 convert_element_type.95
  256.3 0.2 convert_element_type.94
  256.5 0.7 pad_maximum_fusion
  257.2 0.1 multiply_reduce_fusion
  257.3 0.1 reduce_sum.89
  257.4 20.2 %psum.47 = f32[96]{0:T(128)S(1)} all-reduce(f32[96]{0:T(128)S(1)} %reduce_sum.89), channel_id=1, replica_groups=mesh['seq'=8,'tp'=4] {'seq'}, use_global_device_ids=true, to_apply=%region_15.16 | all-reduce | flops 96 | bytes 768 | tf_op jit(solution)/shard_map/psum | solution.py:34
  277.6 66.2 %all-reduce.8.cloned.1.call-done = f32[96,4096]{1,0:T(8,128)} async-done(((f32[96,4096]{1,0:T(8,128)}), f32[96,4096]{1,0:T(8,128)}) %all-reduce.8.cloned.1.call-update) | async-done | bytes 1572880 | tf_op jit(solution)/shard_map/psum | solution.py:34
  343.8 1.8 fusion.32
  345.6 7.5 %all-gather.1 = f32[384,384]{1,0:T(8,128)S(1)} all-gather(f32[96,384]{1,0:T(8,128)S(1)} %fusion.32), channel_id=3, replica_groups=mesh['seq'=8,'tp'=4] {'tp'}, dimensions={0}, use_global_device_ids=true | all-gather | bytes 737280 | tf_op jit(solution)/shard_map/all_gather | solution.py:38
  353.2 0.7 add_convert_fusion.1
  (30 shorter events, 0.3 us)
Async XLA Ops:
  7.2 336.6 %copy-start = (bf16[2048,384]{1,0:T(8,128)(2,1)S(1)}, bf16[2048,384]{1,0:T(8,128)(2,1)}, u32[]{:S(2)}) copy-start(bf16[2048,384]{1,0:T(8,128)(2,1)} %param.24) | copy-start | bytes 4718596
  7.2 4.7 %copy-start.1 = (bf16[4,24,384]{2,1,0:T(8,128)(2,1)S(1)}, bf16[4,24,384]{2,1,0:T(8,128)(2,1)}, u32[]{:S(2)}) copy-start(bf16[4,24,384]{2,1,0:T(8,128)(2,1)} %param.15) | copy-start | bytes 221188
  7.2 4.9 %copy-start.6 = (s32[24]{0:T(128)S(1)}, s32[24]{0:T(128)}, u32[]{:S(2)}) copy-start(s32[24]{0:T(128)} %param.27) | copy-start | bytes 292
  7.2 4.9 %copy-start.4 = (s32[2,16]{1,0:T(2,128)S(1)}, s32[2,16]{1,0:T(2,128)}, u32[]{:S(2)}) copy-start(s32[2,16]{1,0:T(2,128)} %param.28) | copy-start | bytes 388
  7.2 5.0 %copy-start.3 = (s32[24,8]{0,1:T(8,128)S(1)}, s32[24,8]{0,1:T(8,128)}, u32[]{:S(2)}) copy-start(s32[24,8]{0,1:T(8,128)} %param.29) | copy-start | bytes 2308
  7.2 107.2 %all-reduce.4.cloned.1.call-start = ((), (), s32[]{:S(2)}) async-start(), calls=%async_computation | async-start | bytes 1769472 | tf_op jit(solution)/shard_map/psum | solution.py:34
  11.7 230.2 %all-reduce.6.cloned.1.call-start = ((), (), s32[]{:S(2)}) async-start(), calls=%async_computation.1 | async-start | bytes 786432 | tf_op jit(solution)/shard_map/psum | solution.py:140
  91.8 21.8 %copy-start.2 = (s32[24]{0:T(128)S(1)}, s32[24]{0:T(128)}, u32[]{:S(2)}) copy-start(s32[24]{0:T(128)} %param.26) | copy-start | bytes 292
  91.8 21.9 %copy-start.5 = (bf16[384]{0:T(512)(128)(2,1)S(1)}, bf16[384]{0:T(512)(128)(2,1)}, u32[]{:S(2)}) copy-start(bf16[384]{0:T(512)(128)(2,1)} %param.21) | copy-start | bytes 2308
  171.5 172.3 %all-reduce.8.cloned.1.call-start = ((), (), s32[]{:S(2)}) async-start(), calls=%async_computation.2 | async-start | bytes 3145728 | tf_op jit(solution)/shard_map/psum | solution.py:34
Sparse Core Ops, SparseCore 0:
  11.9 78.9 all-reduce.3
  171.6 70.2 all-reduce.5
  256.2 87.5 all-reduce.7
